TPU v7x, 32 devices: a whole 2x2x4 slice. The times are simulated.
32 devices in a mesh: px: 8 (over z, y), py: 4 (over x, core).
Axes of the slice: x: 2, y: 2, z: 4, core: 2. Of those that a mesh axis runs over, the one named last changes fastest.
Arguments:
- spectrum: float32 [2, 1536, 24576], P(None, 'px', 'py'), may hold values from -6 to 6
- concentration: float32 [3072, 24576], P('px', 'py'), may hold values from -6 to 6
- factor_y: float32 [1536, 128], P('py'), may hold values from -0.15625 to 0.15625
- factor_x: float32 [3072, 256], P('px'), may hold values from -0.109375 to 0.109375
Outputs:
- y_compressed: float32 [16, 3072, 128], P('py', 'px')
- core_tensor: float32 [16, 256, 128], P('py', 'px')
All inputs are finite; a program needn't handle non-finite values.
Results may differ from a plain program's by a relative error of at most 0.000076.
Values sent between devices are 32-bit elements; how exact they have to be, the bound alone decides.
No kernel may reach another device: no remote copies, remote signals or barrier semaphores. Data moves between devices by JAX's collectives and lax.ppermute only.
A program may use at most 128 MiB of HBM per device.

v0:
```python
import math
import jax
import jax.numpy as jnp
from jax import lax
from jax.sharding import PartitionSpec as P

NX = 3072
NZ = 16
KX = 1536


def synth_table(first_x, block_width):
    wave = lax.broadcasted_iota(jnp.int32, (KX, block_width), 0)
    column = first_x + lax.broadcasted_iota(jnp.int32, (KX, block_width), 1)
    phase = wave * column % NX
    angle = phase.astype(jnp.float32) * (2.0 * math.pi / NX)
    weight = jnp.where(wave == 0, 1.0, 2.0) / math.sqrt(KX)
    return jnp.concatenate([weight * jnp.cos(angle), -weight * jnp.sin(angle)], axis=0)


def body(spectrum, concentration, factor_y, factor_x):
    x_local = concentration.shape[0]
    line_total = concentration.shape[1]
    y_local = line_total // NZ
    pencil_modes = lax.all_to_all(spectrum, "px", split_axis=2, concat_axis=1, tiled=True)
    line_count = pencil_modes.shape[2]
    stacked_modes = pencil_modes.reshape(2 * KX, line_count)
    block_width = 512
    block_total = NX // block_width

    def fill_block(block_index, velocity):
        first_x = block_index * block_width
        rows = lax.dot_general(
            synth_table(first_x, block_width),
            stacked_modes,
            (((0,), (0,)), ((), ())),
            precision=lax.Precision.HIGHEST,
            preferred_element_type=jnp.float32,
        )
        return lax.dynamic_update_slice_in_dim(velocity, rows, first_x, 0)

    velocity = lax.fori_loop(0, block_total, fill_block, jnp.zeros((NX, line_count), jnp.float32))
    returned = lax.all_to_all(velocity, "px", split_axis=0, concat_axis=1, tiled=True)
    flux_tile = returned * concentration
    flux_cube = flux_tile.reshape(x_local, y_local, NZ)
    rows = flux_cube
    y_compressed = lax.psum_scatter(
        jnp.einsum("xyz,yr->zxr", rows, factor_y, precision=lax.Precision.HIGHEST),
        "py",
        scatter_dimension=0,
        tiled=True,
    )
    core_terms = jnp.einsum("xs,zxr->zsr", factor_x, y_compressed, precision=lax.Precision.HIGHEST)
    core_tensor = lax.psum_scatter(core_terms, "px", scatter_dimension=1, tiled=True)
    return (y_compressed, core_tensor)


def solution(mesh):
    placed = (P(None, "px", "py"), P("px", "py"), P("py", None), P("px", None))
    return jax.shard_map(
        body,
        mesh=mesh,
        in_specs=placed,
        out_specs=(P("py", "px", None), P("py", "px", None)),
        check_vma=False,
    )
```

profile of v0, /device:TPU:0, one launch (start us, length us, event | category | flops | bytes accessed | tf_op | source)
XLA Modules:
  0.0 983.5 jit_solution(7462423224211802599)
XLA Ops:
  7.2 18.4 %copy.17 = f32[2,192,6144]{1,0,2:T(2,128)} copy(f32[2,192,6144]{2,1,0:T(8,128)} %param.6) | data formatting | bytes 18874368 | tf_op args[0]
  25.6 7.3 all-to-all-start
  32.9 273.1 %all-to-all-done = f32[2,192,6144]{1,0,2:T(2,128)} async-done(((f32[2,192,6144]{1,0,2:T(2,128)}), f32[2,192,6144]{1,0,2:T(2,128)}, u32[]{:S(2)}, u32[]{:S(2)}) %all-to-all-start) | async-done | bytes 9437216 | tf_op jit(solution)/shard_map/all_to_all | solution.py:25
  306.0 18.3 %copy.18 = f32[2,8,192,768]{3,2,1,0:T(8,128)} copy(f32[2,8,192,768]{2,0,3,1:T(2,128)} %bitcast.1) | data formatting | bytes 18874368 | tf_op jit(solution)/shard_map/all_to_all | solution.py:25
  324.3 4.2 broadcast_in_dim.15
  328.5 281.5 %while.15 = (s32[]{:T(128)}, f32[3072,768]{1,0:T(8,128)}, f32[3072,768]{1,0:T(8,128)}, s32[]{:T(128)}, s32[]{:T(128)}, /*index=5*/s32[]{:T(128)}, s32[]{:T(128)}) while((s32[]{:T(128)}, f32[3072,768]{1,0:T(8,128)}, f32[3072,768]{1,0:T(8,128)}, s32[]{:T(128)}, s32[]{:T(128)}, /*index=5*/s32[]{:T(128)}, s32[]{:T(128)}) %tuple.56), condition=%wide.region_1.2_spmd, body=%wide.region_0.1_spmd.sunk | while | flops 14505745408 | bytes 23621764 | solution.py:42
  328.5 13.5 %cosine_multiply_fusion.2 = (f32[1536,512]{1,0:T(8,128)S(1)}, f32[1536,512]{1,0:T(8,128)S(1)}) fusion(s32[512]{0:T(512)S(1)} %iota_add_fusion.2, f32[1536]{0:T(1024)S(1)} %get-tuple-element.131, f32[1536]{0:T(1024)S(1)} %get-tuple-element.132), kind=kLoop, calls=%fused_computation.8.clone.1 | loop fusion | flops 8650752 | bytes 6305792 | tf_op jit(solution)/shard_map/while/body/eval_jaxpr/mul | solution.py:18
  342.1 33.4 %fusion.28 = f32[3072,768]{1,0:T(8,128)} fusion(f32[3072,768]{1,0:T(8,128)} %get-tuple-element.143, s32[]{:T(128)S(6)} %select_n.61, f32[3072,768]{1,0:T(8,128)} %get-tuple-element.151, f32[1536,512]{1,0:T(8,128)S(1)} %get-tuple-element.133, f32[1536,512]{1,0:T(8,128)S(1)} %get-tuple-element.134), kind=kOutput, calls=%fused_computation.13.clone.1 | convolution fusion | flops 14497087488 | bytes 17301508 | tf_op jit(solution)/shard_map/while/body/eval_jaxpr/dot_general | solution.py:33
  375.4 13.5 %cosine_multiply_fusion.2 = (f32[1536,512]{1,0:T(8,128)S(1)}, f32[1536,512]{1,0:T(8,128)S(1)}) fusion(s32[512]{0:T(512)S(1)} %iota_add_fusion.2, f32[1536]{0:T(1024)S(1)} %get-tuple-element.131, f32[1536]{0:T(1024)S(1)} %get-tuple-element.132), kind=kLoop, calls=%fused_computation.8.clone.1 | loop fusion | flops 8650752 | bytes 6305792 | tf_op jit(solution)/shard_map/while/body/eval_jaxpr/mul | solution.py:18
  388.9 33.4 %fusion.28 = f32[3072,768]{1,0:T(8,128)} fusion(f32[3072,768]{1,0:T(8,128)} %get-tuple-element.143, s32[]{:T(128)S(6)} %select_n.61, f32[3072,768]{1,0:T(8,128)} %get-tuple-element.151, f32[1536,512]{1,0:T(8,128)S(1)} %get-tuple-element.133, f32[1536,512]{1,0:T(8,128)S(1)} %get-tuple-element.134), kind=kOutput, calls=%fused_computation.13.clone.1 | convolution fusion | flops 14497087488 | bytes 17301508 | tf_op jit(solution)/shard_map/while/body/eval_jaxpr/dot_general | solution.py:33
  422.4 13.5 %cosine_multiply_fusion.2 = (f32[1536,512]{1,0:T(8,128)S(1)}, f32[1536,512]{1,0:T(8,128)S(1)}) fusion(s32[512]{0:T(512)S(1)} %iota_add_fusion.2, f32[1536]{0:T(1024)S(1)} %get-tuple-element.131, f32[1536]{0:T(1024)S(1)} %get-tuple-element.132), kind=kLoop, calls=%fused_computation.8.clone.1 | loop fusion | flops 8650752 | bytes 6305792 | tf_op jit(solution)/shard_map/while/body/eval_jaxpr/mul | solution.py:18
  435.9 33.4 %fusion.28 = f32[3072,768]{1,0:T(8,128)} fusion(f32[3072,768]{1,0:T(8,128)} %get-tuple-element.143, s32[]{:T(128)S(6)} %select_n.61, f32[3072,768]{1,0:T(8,128)} %get-tuple-element.151, f32[1536,512]{1,0:T(8,128)S(1)} %get-tuple-element.133, f32[1536,512]{1,0:T(8,128)S(1)} %get-tuple-element.134), kind=kOutput, calls=%fused_computation.13.clone.1 | convolution fusion | flops 14497087488 | bytes 17301508 | tf_op jit(solution)/shard_map/while/body/eval_jaxpr/dot_general | solution.py:33
  469.3 13.5 %cosine_multiply_fusion.2 = (f32[1536,512]{1,0:T(8,128)S(1)}, f32[1536,512]{1,0:T(8,128)S(1)}) fusion(s32[512]{0:T(512)S(1)} %iota_add_fusion.2, f32[1536]{0:T(1024)S(1)} %get-tuple-element.131, f32[1536]{0:T(1024)S(1)} %get-tuple-element.132), kind=kLoop, calls=%fused_computation.8.clone.1 | loop fusion | flops 8650752 | bytes 6305792 | tf_op jit(solution)/shard_map/while/body/eval_jaxpr/mul | solution.py:18
  482.8 33.4 %fusion.28 = f32[3072,768]{1,0:T(8,128)} fusion(f32[3072,768]{1,0:T(8,128)} %get-tuple-element.143, s32[]{:T(128)S(6)} %select_n.61, f32[3072,768]{1,0:T(8,128)} %get-tuple-element.151, f32[1536,512]{1,0:T(8,128)S(1)} %get-tuple-element.133, f32[1536,512]{1,0:T(8,128)S(1)} %get-tuple-element.134), kind=kOutput, calls=%fused_computation.13.clone.1 | convolution fusion | flops 14497087488 | bytes 17301508 | tf_op jit(solution)/shard_map/while/body/eval_jaxpr/dot_general | solution.py:33
  516.2 13.5 %cosine_multiply_fusion.2 = (f32[1536,512]{1,0:T(8,128)S(1)}, f32[1536,512]{1,0:T(8,128)S(1)}) fusion(s32[512]{0:T(512)S(1)} %iota_add_fusion.2, f32[1536]{0:T(1024)S(1)} %get-tuple-element.131, f32[1536]{0:T(1024)S(1)} %get-tuple-element.132), kind=kLoop, calls=%fused_computation.8.clone.1 | loop fusion | flops 8650752 | bytes 6305792 | tf_op jit(solution)/shard_map/while/body/eval_jaxpr/mul | solution.py:18
  529.7 33.4 %fusion.28 = f32[3072,768]{1,0:T(8,128)} fusion(f32[3072,768]{1,0:T(8,128)} %get-tuple-element.143, s32[]{:T(128)S(6)} %select_n.61, f32[3072,768]{1,0:T(8,128)} %get-tuple-element.151, f32[1536,512]{1,0:T(8,128)S(1)} %get-tuple-element.133, f32[1536,512]{1,0:T(8,128)S(1)} %get-tuple-element.134), kind=kOutput, calls=%fused_computation.13.clone.1 | convolution fusion | flops 14497087488 | bytes 17301508 | tf_op jit(solution)/shard_map/while/body/eval_jaxpr/dot_general | solution.py:33
  563.1 13.5 %cosine_multiply_fusion.2 = (f32[1536,512]{1,0:T(8,128)S(1)}, f32[1536,512]{1,0:T(8,128)S(1)}) fusion(s32[512]{0:T(512)S(1)} %iota_add_fusion.2, f32[1536]{0:T(1024)S(1)} %get-tuple-element.131, f32[1536]{0:T(1024)S(1)} %get-tuple-element.132), kind=kLoop, calls=%fused_computation.8.clone.1 | loop fusion | flops 8650752 | bytes 6305792 | tf_op jit(solution)/shard_map/while/body/eval_jaxpr/mul | solution.py:18
  576.6 33.4 %fusion.28 = f32[3072,768]{1,0:T(8,128)} fusion(f32[3072,768]{1,0:T(8,128)} %get-tuple-element.143, s32[]{:T(128)S(6)} %select_n.61, f32[3072,768]{1,0:T(8,128)} %get-tuple-element.151, f32[1536,512]{1,0:T(8,128)S(1)} %get-tuple-element.133, f32[1536,512]{1,0:T(8,128)S(1)} %get-tuple-element.134), kind=kOutput, calls=%fused_computation.13.clone.1 | convolution fusion | flops 14497087488 | bytes 17301508 | tf_op jit(solution)/shard_map/while/body/eval_jaxpr/dot_general | solution.py:33
  610.1 9.5 copy.19
  619.6 5.0 all-to-all-start.1
  624.7 0.0 reduce-scatter.2.cloned.1.call-start
  624.7 9.6 copy.20
  634.4 195.0 %all-to-all-done.1 = f32[8,384,768]{1,2,0:T(8,128)} async-done(((f32[8,384,768]{1,2,0:T(8,128)}), f32[8,384,768]{1,2,0:T(8,128)}, u32[]{:S(2)}, u32[]{:S(2)}) %all-to-all-start.1) | async-done | bytes 9437216 | tf_op jit(solution)/shard_map/all_to_all | solution.py:43
  829.4 11.2 %bitcast_multiply_fusion = f32[384,6144]{0,1:T(8,128)} fusion(f32[384,6144]{0,1:T(8,128)} %copy.20, f32[8,384,768]{1,2,0:T(8,128)} %all-to-all-done.1), kind=kLoop, calls=%fused_computation.19 | loop fusion | flops 2359296 | bytes 28311552 | tf_op jit(solution)/shard_map/mul | solution.py:44
  840.6 21.0 %fusion.16 = f32[16,384,128]{2,1,0:T(8,128)} fusion(f32[384,384,16]{0,2,1:T(8,128)} %bitcast.26, f32[384,128]{1,0:T(8,128)S(1)} %copy-done.1), kind=kOutput, calls=%fused_computation.22 | convolution fusion | flops 3623878656 | bytes 12779520 | tf_op jit(solution)/shard_map/xyz,yr->zxr/dot_general | solution.py:48
  861.7 37.0 %reduce-scatter.2.cloned.1.call-done = f32[4,384,128]{2,1,0:T(8,128)} async-done(((f32[16,384,128]{2,1,0:T(8,128)}), f32[4,384,128]{2,1,0:T(8,128)}) %reduce-scatter.2.cloned.1.call-update) | async-done | bytes 786448 | tf_op jit(solution)/shard_map/reduce_scatter | solution.py:47
  898.8 2.6 convolution_bitcast_fusion
  901.3 1.0 copy.23
  902.3 0.6 dynamic-slice
  903.6 71.6 %all-reduce.3.cloned.1.call-done = f32[4,256,128]{2,0,1:T(4,128)} async-done(((f32[4,256,128]{2,0,1:T(4,128)}), f32[4,256,128]{2,0,1:T(4,128)}) %all-reduce.3.cloned.1.call-update) | async-done | bytes 524304
  975.2 0.8 constant_dynamic-slice_fusion
  976.1 0.6 copy.24
  (21 shorter events, 0.1 us)
Async XLA Ops:
  7.2 891.6 %copy-start = (f32[384,256]{1,0:T(8,128)S(1)}, f32[384,256]{1,0:T(8,128)}, u32[]{:S(2)}) copy-start(f32[384,256]{1,0:T(8,128)} %param.9) | copy-start | bytes 1179652
  25.6 280.4 %all-to-all-start = ((f32[2,192,6144]{1,0,2:T(2,128)}), f32[2,192,6144]{1,0,2:T(2,128)}, u32[]{:S(2)}, u32[]{:S(2)}) async-start(f32[2,192,6144]{1,0,2:T(2,128)} %copy.17), calls=%async_computation | async-start | bytes 25165824 | tf_op jit(solution)/shard_map/all_to_all | solution.py:25
  619.6 209.8 %all-to-all-start.1 = ((f32[8,384,768]{1,2,0:T(8,128)}), f32[8,384,768]{1,2,0:T(8,128)}, u32[]{:S(2)}, u32[]{:S(2)}) async-start(f32[8,384,768]{1,2,0:T(8,128)} %copy.19), calls=%async_computation.1 | async-start | bytes 18874368 | tf_op jit(solution)/shard_map/all_to_all | solution.py:43
  624.7 274.1 %reduce-scatter.2.cloned.1.call-start = ((), (), s32[]{:S(2)}) async-start(), calls=%async_computation.3 | async-start | bytes 3932160 | tf_op jit(solution)/shard_map/reduce_scatter | solution.py:47
  634.4 206.3 %copy-start.1 = (f32[384,128]{1,0:T(8,128)S(1)}, f32[384,128]{1,0:T(8,128)}, u32[]{:S(2)}) copy-start(f32[384,128]{1,0:T(8,128)} %param.8) | copy-start | bytes 589828
  861.6 40.7 %copy-start.2 = (u32[32]{0:T(128)S(1)}, u32[32]{0:T(128)}, u32[]{:S(2)}) copy-start(u32[32]{0:T(128)} %constant.99) | copy-start | bytes 388
  861.7 113.6 %all-reduce.3.cloned.1.call-start = ((), (), s32[]{:S(2)}) async-start(), calls=%async_computation.4 | async-start | bytes 1048576
Sparse Core Ops, SparseCore 0:
  861.8 36.9 reduce-scatter.1
  902.5 72.7 all-reduce.2
where the time goes:
time: 985 us; the launch traced here: 984 us
  waiting for transfers between devices  577 us (59%)
  matrix products  224 us (23%)
  other arithmetic  92.3 us (9%)
  local copies, waits for them, and re-layouts  63.2 us (6%)
  between operations  14.7 us (1%)
  starting transfers between devices  12.4 us (1%)
    all_to_all x1, waiting for transfers between devices, body(): lax.all_to_all(spectrum, 'px', split_axis=2, concat_axis=1, tiled=True)  273 us
    dot_general x6, matrix products, fill_block(): lax.dot_general(synth_table(first_x, block_width), stacked_modes, (((0,),...  200 us
    all_to_all x1, waiting for transfers between devices, body(): lax.all_to_all(velocity, 'px', split_axis=0, concat_axis=1, tiled=True)  195 us
    mul x6, other arithmetic, synth_table(): weight * jnp.cos(angle)  81 us
    unnamed x3, waiting for transfers between devices  71.7 us
    reduce_scatter x1, waiting for transfers between devices, body(): lax.psum_scatter(jnp.einsum('xyz,yr->zxr', rows, factor_y, precision=lax....  37 us
    unnamed x11, local copies, waits for them, and re-layouts  30.1 us
    dot_general x1, matrix products, body(): jnp.einsum('xyz,yr->zxr', rows, factor_y, precision=lax.Precision.HIGHEST)  21 us
  transfers between devices with their start and end apart: 4, of which 4 were waited for; matrix products, arithmetic and copies ran while one was open for 1% of the time, Pallas kernels for 0%

commit v1 on v0

--- a/solution.py
+++ b/solution.py
@@ -22,7 +22,24 @@
     x_local = concentration.shape[0]
     line_total = concentration.shape[1]
     y_local = line_total // NZ
-    pencil_modes = lax.all_to_all(spectrum, "px", split_axis=2, concat_axis=1, tiled=True)
+    oldest = lax.axis_index("px")
+    newest = lax.axis_size("px")
+    carry, e_next = (newest, oldest)
+    base_arr = list(spectrum.shape)
+    value_now = spectrum.shape[2] // carry
+    base_arr[2] = value_now
+    last = base_arr[1]
+    base_arr[1] = last * carry
+    pencil_modes = jnp.zeros(base_arr, spectrum.dtype)
+    b = 0
+    while b < carry:
+        work_now = lax.dynamic_slice_in_dim(spectrum, (e_next ^ b) * value_now, value_now, axis=2)
+        if b:
+            work_now = lax.ppermute(work_now, "px", [(nth, nth ^ b) for nth in range(carry)])
+        pencil_modes = lax.dynamic_update_slice_in_dim(
+            pencil_modes, work_now, (e_next ^ b) * last, axis=1
+        )
+        b = b + 1
     line_count = pencil_modes.shape[2]
     stacked_modes = pencil_modes.reshape(2 * KX, line_count)
     block_width = 512

time: 985 us -> 889 us (0.903)
  waiting for transfers between devices: 577 us -> 443 us
  starting transfers between devices: 12.4 us -> 61.1 us
  local copies, waits for them, and re-layouts: 63.2 us -> 53.1 us
    all_to_all x1 -> x0, waiting for transfers between devices: 273 us -> none  [body(): lax.all_to_all(spectrum, 'px', split_axis=2, concat_axis=1, tiled=True)]
    ppermute x0 -> x7, waiting for transfers between devices: none -> 140 us  [body(): lax.ppermute(work_now, 'px', [(nth, nth ^ b) for nth in range(carry)])]
    all_to_all x1, starting transfers between devices: 5.04 us -> 47.6 us  [body(): lax.all_to_all(velocity, 'px', split_axis=0, concat_axis=1, tiled=True)]
    all_to_all x1 -> x0, local copies, waits for them, and re-layouts: 18.3 us -> none  [body(): lax.all_to_all(spectrum, 'px', split_axis=2, concat_axis=1, tiled=True)]
    unnamed x11 -> x18, local copies, waits for them, and re-layouts: 30.1 us -> 14.5 us
    dynamic_update_slice x0 -> x7, local copies, waits for them, and re-layouts: none -> 15.5 us  [body(): lax.dynamic_update_slice_in_dim(pencil_modes, work_now, (e_next ^ b) * la...]
    ppermute x0 -> x7, starting transfers between devices: none -> 13.4 us  [body(): lax.ppermute(work_now, 'px', [(nth, nth ^ b) for nth in range(carry)])]
  transfers between devices with their start and end apart: 4 -> 10, of which waited for: 4 -> 7; matrix products, arithmetic and copies ran while one was open for 1% -> 3% of each run, Pallas kernels for 0% -> 0%
where the time goes in v1:
time: 889 us; the launch traced here: 888 us
  waiting for transfers between devices  443 us (50%)
  matrix products  224 us (25%)
  other arithmetic  92.3 us (10%)
  starting transfers between devices  61.1 us (7%)
  local copies, waits for them, and re-layouts  53.1 us (6%)
  between operations  14.8 us (2%)
    dot_general x6, matrix products, fill_block(): lax.dot_general(synth_table(first_x, block_width), stacked_modes, (((0,),...  200 us
    all_to_all x1, waiting for transfers between devices, body(): lax.all_to_all(velocity, 'px', split_axis=0, concat_axis=1, tiled=True)  196 us
    ppermute x7, waiting for transfers between devices, body(): lax.ppermute(work_now, 'px', [(nth, nth ^ b) for nth in range(carry)])  140 us
    mul x6, other arithmetic, synth_table(): weight * jnp.cos(angle)  81 us
    unnamed x3, waiting for transfers between devices  71.7 us
    all_to_all x1, starting transfers between devices, body(): lax.all_to_all(velocity, 'px', split_axis=0, concat_axis=1, tiled=True)  47.6 us
    reduce_scatter x1, waiting for transfers between devices, body(): lax.psum_scatter(jnp.einsum('xyz,yr->zxr', rows, factor_y, precision=lax....  35.4 us
    dot_general x1, matrix products, body(): jnp.einsum('xyz,yr->zxr', rows, factor_y, precision=lax.Precision.HIGHEST)  21 us
  transfers between devices with their start and end apart: 10, of which 7 were waited for; matrix products, arithmetic and copies ran while one was open for 3% of the time, Pallas kernels for 0%

profile of v1, /device:TPU:0, one launch (start us, length us, event | category | flops | bytes accessed | tf_op | source)
XLA Modules:
  0.0 888.2 jit_solution(16352437532129284215)
XLA Ops:
  7.2 5.4 broadcast_in_dim.19
  14.4 2.8 constant_dynamic-slice_fusion
  17.2 3.0 collective-permute-start
  21.7 3.0 collective-permute-start.3
  26.1 20.1 %collective-permute-done = f32[2,192,768]{2,1,0:T(8,128)S(1)} collective-permute-done((f32[2,192,768]{2,1,0:T(8,128)S(1)}, f32[2,192,768]{2,1,0:T(8,128)S(1)}, u32[]{:S(2)}, u32[]{:S(2)}) %collective-permute-start) | collective-permute-done | bytes 1179680 | tf_op jit(solution)/shard_map/ppermute | solution.py:38
  46.2 3.8 collective-permute-start.5
  50.0 48.7 %collective-permute-done.1 = f32[2,192,768]{2,1,0:T(8,128)S(1)} collective-permute-done((f32[2,192,768]{2,1,0:T(8,128)S(1)}, f32[2,192,768]{2,1,0:T(8,128)S(1)}, u32[]{:S(2)}, u32[]{:S(2)}) %collective-permute-start.1) | collective-permute-done | bytes 1179680 | tf_op jit(solution)/shard_map/ppermute | solution.py:38
  104.0 17.6 %collective-permute-done.2 = f32[2,192,768]{2,1,0:T(8,128)} collective-permute-done((f32[2,192,768]{2,1,0:T(8,128)}, f32[2,192,768]{2,1,0:T(8,128)}, u32[]{:S(2)}, u32[]{:S(2)}) %collective-permute-start.2) | collective-permute-done | bytes 1179680 | tf_op jit(solution)/shard_map/ppermute | solution.py:38
  126.3 53.3 %collective-permute-done.4 = f32[2,192,768]{2,1,0:T(8,128)} collective-permute-done((f32[2,192,768]{2,1,0:T(8,128)}, f32[2,192,768]{2,1,0:T(8,128)}, u32[]{:S(2)}, u32[]{:S(2)}) %collective-permute-start.4) | collective-permute-done | bytes 1179680 | tf_op jit(solution)/shard_map/ppermute | solution.py:38
  186.8 4.3 broadcast_in_dim.18
  191.1 281.5 %while.15 = (s32[]{:T(128)}, f32[3072,768]{1,0:T(8,128)}, f32[3072,768]{1,0:T(8,128)}, s32[]{:T(128)}, s32[]{:T(128)}, /*index=5*/s32[]{:T(128)}, s32[]{:T(128)}) while((s32[]{:T(128)}, f32[3072,768]{1,0:T(8,128)}, f32[3072,768]{1,0:T(8,128)}, s32[]{:T(128)}, s32[]{:T(128)}, /*index=5*/s32[]{:T(128)}, s32[]{:T(128)}) %tuple.56), condition=%wide.region_1.2_spmd, body=%wide.region_0.1_spmd.sunk | while | flops 14505745408 | bytes 23621764 | solution.py:59
  191.1 13.5 %cosine_multiply_fusion.2 = (f32[1536,512]{1,0:T(8,128)S(1)}, f32[1536,512]{1,0:T(8,128)S(1)}) fusion(s32[512]{0:T(512)S(1)} %iota_add_fusion.2, f32[1536]{0:T(1024)S(1)} %get-tuple-element.139, f32[1536]{0:T(1024)S(1)} %get-tuple-element.140), kind=kLoop, calls=%fused_computation.8.clone.1 | loop fusion | flops 8650752 | bytes 6305792 | tf_op jit(solution)/shard_map/while/body/eval_jaxpr/mul | solution.py:18
  204.7 33.4 %fusion.28 = f32[3072,768]{1,0:T(8,128)} fusion(f32[3072,768]{1,0:T(8,128)} %get-tuple-element.151, s32[]{:T(128)S(6)} %select_n.125, f32[3072,768]{1,0:T(8,128)} %get-tuple-element.159, f32[1536,512]{1,0:T(8,128)S(1)} %get-tuple-element.141, f32[1536,512]{1,0:T(8,128)S(1)} %get-tuple-element.142), kind=kOutput, calls=%fused_computation.13.clone.1 | convolution fusion | flops 14497087488 | bytes 17301508 | tf_op jit(solution)/shard_map/while/body/eval_jaxpr/dot_general | solution.py:50
  238.0 13.5 %cosine_multiply_fusion.2 = (f32[1536,512]{1,0:T(8,128)S(1)}, f32[1536,512]{1,0:T(8,128)S(1)}) fusion(s32[512]{0:T(512)S(1)} %iota_add_fusion.2, f32[1536]{0:T(1024)S(1)} %get-tuple-element.139, f32[1536]{0:T(1024)S(1)} %get-tuple-element.140), kind=kLoop, calls=%fused_computation.8.clone.1 | loop fusion | flops 8650752 | bytes 6305792 | tf_op jit(solution)/shard_map/while/body/eval_jaxpr/mul | solution.py:18
  251.6 33.4 %fusion.28 = f32[3072,768]{1,0:T(8,128)} fusion(f32[3072,768]{1,0:T(8,128)} %get-tuple-element.151, s32[]{:T(128)S(6)} %select_n.125, f32[3072,768]{1,0:T(8,128)} %get-tuple-element.159, f32[1536,512]{1,0:T(8,128)S(1)} %get-tuple-element.141, f32[1536,512]{1,0:T(8,128)S(1)} %get-tuple-element.142), kind=kOutput, calls=%fused_computation.13.clone.1 | convolution fusion | flops 14497087488 | bytes 17301508 | tf_op jit(solution)/shard_map/while/body/eval_jaxpr/dot_general | solution.py:50
  284.9 13.5 %cosine_multiply_fusion.2 = (f32[1536,512]{1,0:T(8,128)S(1)}, f32[1536,512]{1,0:T(8,128)S(1)}) fusion(s32[512]{0:T(512)S(1)} %iota_add_fusion.2, f32[1536]{0:T(1024)S(1)} %get-tuple-element.139, f32[1536]{0:T(1024)S(1)} %get-tuple-element.140), kind=kLoop, calls=%fused_computation.8.clone.1 | loop fusion | flops 8650752 | bytes 6305792 | tf_op jit(solution)/shard_map/while/body/eval_jaxpr/mul | solution.py:18
  298.5 33.4 %fusion.28 = f32[3072,768]{1,0:T(8,128)} fusion(f32[3072,768]{1,0:T(8,128)} %get-tuple-element.151, s32[]{:T(128)S(6)} %select_n.125, f32[3072,768]{1,0:T(8,128)} %get-tuple-element.159, f32[1536,512]{1,0:T(8,128)S(1)} %get-tuple-element.141, f32[1536,512]{1,0:T(8,128)S(1)} %get-tuple-element.142), kind=kOutput, calls=%fused_computation.13.clone.1 | convolution fusion | flops 14497087488 | bytes 17301508 | tf_op jit(solution)/shard_map/while/body/eval_jaxpr/dot_general | solution.py:50
  331.9 13.5 %cosine_multiply_fusion.2 = (f32[1536,512]{1,0:T(8,128)S(1)}, f32[1536,512]{1,0:T(8,128)S(1)}) fusion(s32[512]{0:T(512)S(1)} %iota_add_fusion.2, f32[1536]{0:T(1024)S(1)} %get-tuple-element.139, f32[1536]{0:T(1024)S(1)} %get-tuple-element.140), kind=kLoop, calls=%fused_computation.8.clone.1 | loop fusion | flops 8650752 | bytes 6305792 | tf_op jit(solution)/shard_map/while/body/eval_jaxpr/mul | solution.py:18
  345.4 33.4 %fusion.28 = f32[3072,768]{1,0:T(8,128)} fusion(f32[3072,768]{1,0:T(8,128)} %get-tuple-element.151, s32[]{:T(128)S(6)} %select_n.125, f32[3072,768]{1,0:T(8,128)} %get-tuple-element.159, f32[1536,512]{1,0:T(8,128)S(1)} %get-tuple-element.141, f32[1536,512]{1,0:T(8,128)S(1)} %get-tuple-element.142), kind=kOutput, calls=%fused_computation.13.clone.1 | convolution fusion | flops 14497087488 | bytes 17301508 | tf_op jit(solution)/shard_map/while/body/eval_jaxpr/dot_general | solution.py:50
  378.8 13.5 %cosine_multiply_fusion.2 = (f32[1536,512]{1,0:T(8,128)S(1)}, f32[1536,512]{1,0:T(8,128)S(1)}) fusion(s32[512]{0:T(512)S(1)} %iota_add_fusion.2, f32[1536]{0:T(1024)S(1)} %get-tuple-element.139, f32[1536]{0:T(1024)S(1)} %get-tuple-element.140), kind=kLoop, calls=%fused_computation.8.clone.1 | loop fusion | flops 8650752 | bytes 6305792 | tf_op jit(solution)/shard_map/while/body/eval_jaxpr/mul | solution.py:18
  392.3 33.4 %fusion.28 = f32[3072,768]{1,0:T(8,128)} fusion(f32[3072,768]{1,0:T(8,128)} %get-tuple-element.151, s32[]{:T(128)S(6)} %select_n.125, f32[3072,768]{1,0:T(8,128)} %get-tuple-element.159, f32[1536,512]{1,0:T(8,128)S(1)} %get-tuple-element.141, f32[1536,512]{1,0:T(8,128)S(1)} %get-tuple-element.142), kind=kOutput, calls=%fused_computation.13.clone.1 | convolution fusion | flops 14497087488 | bytes 17301508 | tf_op jit(solution)/shard_map/while/body/eval_jaxpr/dot_general | solution.py:50
  425.7 13.5 %cosine_multiply_fusion.2 = (f32[1536,512]{1,0:T(8,128)S(1)}, f32[1536,512]{1,0:T(8,128)S(1)}) fusion(s32[512]{0:T(512)S(1)} %iota_add_fusion.2, f32[1536]{0:T(1024)S(1)} %get-tuple-element.139, f32[1536]{0:T(1024)S(1)} %get-tuple-element.140), kind=kLoop, calls=%fused_computation.8.clone.1 | loop fusion | flops 8650752 | bytes 6305792 | tf_op jit(solution)/shard_map/while/body/eval_jaxpr/mul | solution.py:18
  439.2 33.4 %fusion.28 = f32[3072,768]{1,0:T(8,128)} fusion(f32[3072,768]{1,0:T(8,128)} %get-tuple-element.151, s32[]{:T(128)S(6)} %select_n.125, f32[3072,768]{1,0:T(8,128)} %get-tuple-element.159, f32[1536,512]{1,0:T(8,128)S(1)} %get-tuple-element.141, f32[1536,512]{1,0:T(8,128)S(1)} %get-tuple-element.142), kind=kOutput, calls=%fused_computation.13.clone.1 | convolution fusion | flops 14497087488 | bytes 17301508 | tf_op jit(solution)/shard_map/while/body/eval_jaxpr/dot_general | solution.py:50
  472.7 9.6 %copy.15 = f32[8,384,768]{1,2,0:T(8,128)} copy(f32[8,384,768]{2,1,0:T(8,128)} %bitcast.23) | data formatting | bytes 18874368 | tf_op jit(solution)/shard_map/all_to_all | solution.py:60
  482.3 47.6 %all-to-all-start = ((f32[8,384,768]{1,2,0:T(8,128)}), f32[8,384,768]{1,2,0:T(8,128)}, u32[]{:S(2)}, u32[]{:S(2)}) async-start(f32[8,384,768]{1,2,0:T(8,128)} %copy.15), calls=%async_computation | async-start | bytes 18874368 | tf_op jit(solution)/shard_map/all_to_all | solution.py:60
  529.9 9.6 %copy.16 = f32[384,6144]{0,1:T(8,128)} copy(f32[384,6144]{1,0:T(8,128)} %param.7) | data formatting | bytes 18874368 | tf_op args[1]
  539.6 195.9 %all-to-all-done = f32[8,384,768]{1,2,0:T(8,128)} async-done(((f32[8,384,768]{1,2,0:T(8,128)}), f32[8,384,768]{1,2,0:T(8,128)}, u32[]{:S(2)}, u32[]{:S(2)}) %all-to-all-start) | async-done | bytes 9437216 | tf_op jit(solution)/shard_map/all_to_all | solution.py:60
  735.5 11.3 %bitcast_multiply_fusion = f32[384,6144]{0,1:T(8,128)} fusion(f32[384,6144]{0,1:T(8,128)} %copy.16, f32[8,384,768]{1,2,0:T(8,128)} %all-to-all-done), kind=kLoop, calls=%fused_computation.19 | loop fusion | flops 2359296 | bytes 28311552 | tf_op jit(solution)/shard_map/mul | solution.py:61
  746.8 21.0 %fusion.16 = f32[16,384,128]{2,1,0:T(8,128)} fusion(f32[384,384,16]{0,2,1:T(8,128)} %bitcast.22, f32[384,128]{1,0:T(8,128)S(1)} %copy-done.5), kind=kOutput, calls=%fused_computation.22 | convolution fusion | flops 3623878656 | bytes 12779520 | tf_op jit(solution)/shard_map/xyz,yr->zxr/dot_general | solution.py:65
  767.9 35.4 %reduce-scatter.2.cloned.1.call-done = f32[4,384,128]{2,1,0:T(8,128)} async-done(((f32[16,384,128]{2,1,0:T(8,128)}), f32[4,384,128]{2,1,0:T(8,128)}) %reduce-scatter.2.cloned.1.call-update) | async-done | bytes 786448 | tf_op jit(solution)/shard_map/reduce_scatter | solution.py:64
  803.3 2.6 convolution_bitcast_fusion
  808.2 71.7 %all-reduce.3.cloned.1.call-done = f32[4,256,128]{2,0,1:T(4,128)} async-done(((f32[4,256,128]{2,0,1:T(4,128)}), f32[4,256,128]{2,0,1:T(4,128)}) %all-reduce.3.cloned.1.call-update) | async-done | bytes 524304
  (48 shorter events, 25.1 us)
Async XLA Ops:
  7.2 796.1 %copy-start = (f32[384,256]{1,0:T(8,128)S(1)}, f32[384,256]{1,0:T(8,128)}, u32[]{:S(2)}) copy-start(f32[384,256]{1,0:T(8,128)} %param.9) | copy-start | bytes 1179652
  7.2 7.1 copy-start.1
  17.2 29.0 %collective-permute-start = (f32[2,192,768]{2,1,0:T(8,128)S(1)}, f32[2,192,768]{2,1,0:T(8,128)S(1)}, u32[]{:S(2)}, u32[]{:S(2)}) collective-permute-start(f32[2,192,768]{2,1,0:T(8,128)S(1)} %get-tuple-element.113), channel_id=1, source_target_pairs={{0,4},{4,0},{8,12},{12,8},{16,20},{20,16},{24,28},{28,24},{1,5},{5... | collective-permute-start | bytes 3538952 | tf_op jit(solution)/shard_map/ppermute | solution.py:38
  20.2 78.4 %collective-permute-start.1 = (f32[2,192,768]{2,1,0:T(8,128)S(1)}, f32[2,192,768]{2,1,0:T(8,128)S(1)}, u32[]{:S(2)}, u32[]{:S(2)}) collective-permute-start(f32[2,192,768]{2,1,0:T(8,128)S(1)} %get-tuple-element.112), channel_id=1, source_target_pairs={{0,8},{4,12},{8,0},{12,4},{16,24},{20,28},{24,16},{28,20},{1,9},{5... | collective-permute-start | bytes 3538952 | tf_op jit(solution)/shard_map/ppermute | solution.py:38
  21.7 99.9 %collective-permute-start.2 = (f32[2,192,768]{2,1,0:T(8,128)}, f32[2,192,768]{2,1,0:T(8,128)}, u32[]{:S(2)}, u32[]{:S(2)}) collective-permute-start(f32[2,192,768]{2,1,0:T(8,128)} %get-tuple-element.111), channel_id=1, source_target_pairs={{0,12},{4,8},{8,4},{12,0},{16,28},{20,24},{24,20},{28,16},{1,13},{... | collective-permute-start | bytes 3538952 | tf_op jit(solution)/shard_map/ppermute | solution.py:38
  21.7 102.2 %collective-permute-start.3 = (f32[2,192,768]{2,1,0:T(8,128)}, f32[2,192,768]{2,1,0:T(8,128)}, u32[]{:S(2)}, u32[]{:S(2)}) collective-permute-start(f32[2,192,768]{2,1,0:T(8,128)} %get-tuple-element.110), channel_id=1, source_target_pairs={{0,16},{4,20},{8,24},{12,28},{16,0},{20,4},{24,8},{28,12},{1,17},{... | collective-permute-start | bytes 3538952 | tf_op jit(solution)/shard_map/ppermute | solution.py:38
  24.7 154.9 %collective-permute-start.4 = (f32[2,192,768]{2,1,0:T(8,128)}, f32[2,192,768]{2,1,0:T(8,128)}, u32[]{:S(2)}, u32[]{:S(2)}) collective-permute-start(f32[2,192,768]{2,1,0:T(8,128)} %get-tuple-element.109), channel_id=1, source_target_pairs={{0,20},{4,16},{8,28},{12,24},{16,4},{20,0},{24,12},{28,8},{1,21},{... | collective-permute-start | bytes 3538952 | tf_op jit(solution)/shard_map/ppermute | solution.py:38
  46.2 52.4 %copy-start.2 = (f32[2,192,768]{2,1,0:T(8,128)}, f32[2,192,768]{2,1,0:T(8,128)S(1)}, u32[]{:S(2)}) copy-start(f32[2,192,768]{2,1,0:T(8,128)S(1)} %collective-permute-done) | copy-start | bytes 3538948
  46.2 135.8 %collective-permute-start.5 = (f32[2,192,768]{2,1,0:T(8,128)S(1)}, f32[2,192,768]{2,1,0:T(8,128)}, u32[]{:S(2)}, u32[]{:S(2)}) collective-permute-start(f32[2,192,768]{2,1,0:T(8,128)S(1)} %get-tuple-element.115), channel_id=1, source_target_pairs={{0,24},{4,28},{8,16},{12,20},{16,8},{20,12},{24,0},{28,4},{1,25},{... | collective-permute-start | bytes 3538952 | tf_op jit(solution)/shard_map/ppermute | solution.py:38
  98.6 1.0 copy-start.3
  99.6 84.8 %collective-permute-start.6 = (f32[2,192,768]{2,1,0:T(8,128)S(1)}, f32[2,192,768]{2,1,0:T(8,128)}, u32[]{:S(2)}, u32[]{:S(2)}) collective-permute-start(f32[2,192,768]{2,1,0:T(8,128)S(1)} %get-tuple-element.108), channel_id=1, source_target_pairs={{0,28},{4,24},{8,20},{12,16},{16,12},{20,8},{24,4},{28,0},{1,29},{... | collective-permute-start | bytes 3538952 | tf_op jit(solution)/shard_map/ppermute | solution.py:38
  100.4 2.5 copy-start.4
  482.3 253.3 %all-to-all-start = ((f32[8,384,768]{1,2,0:T(8,128)}), f32[8,384,768]{1,2,0:T(8,128)}, u32[]{:S(2)}, u32[]{:S(2)}) async-start(f32[8,384,768]{1,2,0:T(8,128)} %copy.15), calls=%async_computation | async-start | bytes 18874368 | tf_op jit(solution)/shard_map/all_to_all | solution.py:60
  529.9 273.4 %reduce-scatter.2.cloned.1.call-start = ((), (), s32[]{:S(2)}) async-start(), calls=%async_computation.2 | async-start | bytes 3932160 | tf_op jit(solution)/shard_map/reduce_scatter | solution.py:64
  539.6 207.2 %copy-start.5 = (f32[384,128]{1,0:T(8,128)S(1)}, f32[384,128]{1,0:T(8,128)}, u32[]{:S(2)}) copy-start(f32[384,128]{1,0:T(8,128)} %param.8) | copy-start | bytes 589828
  767.8 39.1 %copy-start.6 = (u32[32]{0:T(128)S(1)}, u32[32]{0:T(128)}, u32[]{:S(2)}) copy-start(u32[32]{0:T(128)} %constant.128) | copy-start | bytes 388
  767.8 112.0 %all-reduce.3.cloned.1.call-start = ((), (), s32[]{:S(2)}) async-start(), calls=%async_computation.3 | async-start | bytes 1048576
Sparse Core Ops, SparseCore 0:
  768.0 35.2 reduce-scatter.1
  807.0 72.7 all-reduce.2
